TPU v7x, 32 devices: a whole 2x2x4 slice. The times are simulated.
32 devices in a mesh: group: 2 (over y), section: 4 (over z), span: 2 (over x), mp: 2 (over core).
Axes of the slice: x: 2, y: 2, z: 4, core: 2. Of those that a mesh axis runs over, the one named last changes fastest.
Arguments:
- queries: bfloat16 [8, 256, 4096], P(('group', 'section'), None, ('span', 'mp')), parts along dimension 0, may hold values from -5 to 5
- keys_values: bfloat16 [2, 8, 256, 4096], P(None, ('group', 'section'), None, ('span', 'mp')), parts along dimension 1, may hold values from -5 to 5
- latents: bfloat16 [8, 256, 5120], P(('group', 'section'), ('span', 'mp')), parts along dimension 0, may hold values from -6 to 6
- out_weight: bfloat16 [4096, 5120], P(('span', 'mp')), may hold values from -3 to 3
- gate_table: float32 [8, 5120], replicated, may hold values from 0.5 to 1.5
- level_index: int32 [8], P(('group', 'section')), parts along dimension 0, may hold values from 0 to 7
- pair_window: int32 [6], P('group'), parts along dimension 0, may hold values from 0 to 256
Outputs:
- shifted: bfloat16 [8, 256, 5120], P(('group', 'section'), ('span', 'mp')), parts along dimension 0
There are 2 independent parts, one for each index of `group`. A program takes and returns all parts, laid end to end along the dimension named above; an argument that names none is the same for every part. Nothing has to cross between parts.
All inputs are finite; a program needn't handle non-finite values.
Results may differ from a plain program's by a relative error of at most 0.015.
Values may be sent and summed in bfloat16 or wider, within the bound.
A program may use at most 64 MiB of HBM per device.

v0:
```python
import functools
import math

import jax
import jax.numpy as jnp
from jax import lax
from jax.experimental import pallas as pl
from jax.experimental.pallas import tpu as pltpu
from jax.sharding import PartitionSpec as P

HD = 128
NEG_BIG = -1e30
CHUNK = 256
LAG_MP = 3
LAG_SPAN = 8


def fused(
    sections, spans, mps, chunk, lag_mp, lag_span,
    level_hbm, window_hbm, q_hbm, kv_hbm, lat_hbm, w_hbm, gate_hbm, out_hbm,
    q_buf, kv_buf, lat_buf, w_buf, gate_buf, below, above, att, keep,
    send_mp, recv_mp, send_span, recv_span, send_next,
    level_ref, window_ref, load_sems, up_send, up_recv, down_send, down_recv,
    mp_send, mp_recv, span_send, span_recv, next_send, next_recv, relay,
):
    s = lax.axis_index("section")
    x = lax.axis_index("span")
    m = lax.axis_index("mp")
    last = sections - 1
    heads = below.shape[0]
    tokens = kv_buf.shape[1]
    width = kv_buf.shape[2]
    rows = lat_buf.shape[0]
    chunks = keep.shape[0]
    succ = lax.rem(s + 1, sections)
    pred = lax.rem(s + sections - 1, sections)

    barrier = pltpu.get_barrier_semaphore()

    @pl.when(s < last)
    def _():
        pl.semaphore_signal(barrier, 1, device_id={"section": succ})

    @pl.when(s > 0)
    def _():
        pl.semaphore_signal(barrier, 1, device_id={"section": pred})

    for j in range(1, mps):
        pl.semaphore_signal(barrier, 1, device_id={"mp": lax.rem(m + j, mps)})
    for i in range(1, spans):
        pl.semaphore_signal(barrier, 1, device_id={"span": lax.rem(x + i, spans)})
    others = mps - 1 + spans - 1

    windows = pltpu.make_async_copy(window_hbm, window_ref, load_sems.at[6])
    loads = [
        pltpu.make_async_copy(q_hbm.at[0], q_buf, load_sems.at[0]),
        pltpu.make_async_copy(kv_hbm.at[:, 0], kv_buf, load_sems.at[1]),
        pltpu.make_async_copy(lat_hbm.at[0], lat_buf, load_sems.at[2]),
        pltpu.make_async_copy(gate_hbm, gate_buf, load_sems.at[3]),
        pltpu.make_async_copy(w_hbm, w_buf, load_sems.at[4]),
        pltpu.make_async_copy(level_hbm, level_ref, load_sems.at[5]),
    ]

    @pl.when((s > 0) & (s < last))
    def _():
        pl.semaphore_wait(barrier, others + 2)

    @pl.when((s == 0) | (s == last))
    def _():
        pl.semaphore_wait(barrier, others + 1)

    def head_cols(h):
        return pl.ds(pl.multiple_of(h * HD, HD), HD)

    def chunk_cols(c):
        return pl.ds(pl.multiple_of(c * chunk, chunk), chunk)

    def up(h):
        return pltpu.make_async_remote_copy(
            kv_hbm.at[:, 0, :, head_cols(h)], below.at[h], up_send.at[h], up_recv.at[h],
            device_id={"section": succ},
        )

    def down(h):
        return pltpu.make_async_remote_copy(
            kv_hbm.at[:, 0, :, head_cols(h)], above.at[h], down_send.at[h], down_recv.at[h],
            device_id={"section": pred},
        )

    @pl.loop(0, heads)
    def _(h):
        @pl.when(s < last)
        def _():
            up(h).start()

    @pl.loop(0, heads)
    def _(h):
        @pl.when(s > 0)
        def _():
            down(h).start()

    windows.start()
    for load in loads:
        load.start()

    @pl.when(s == 0)
    def _():
        below[...] = jnp.zeros_like(below)
        pl.semaphore_signal(relay, 1, device_id={"section": succ})

    @pl.when(s == last)
    def _():
        above[...] = jnp.zeros_like(above)

    windows.wait()
    pairs = window_ref.shape[0]
    w_lo = jnp.where(s > 0, window_ref[jnp.clip(s - 1, 0, pairs - 1)], 0)
    w_hi = jnp.where(s < last, window_ref[jnp.clip(s, 0, pairs - 1)], 0)
    key_ids = lax.broadcasted_iota(jnp.int32, (1, tokens), 1)
    mask_lo = key_ids >= tokens - w_lo
    mask_hi = key_ids < w_hi
    scale = 1.0 / math.sqrt(HD)
    loads[0].wait()
    loads[1].wait()

    def score(q, k):
        return lax.dot_general(
            q, k, (((1,), (1,)), ((), ())), preferred_element_type=jnp.float32
        ) * scale

    @pl.loop(0, heads)
    def _(h):
        cols = head_cols(h)
        q = q_buf[:, cols]
        s_own = score(q, kv_buf[0, :, cols])

        @pl.when(s > 0)
        def _():
            up(h).wait_recv()

        @pl.when(s < last)
        def _():
            down(h).wait_recv()

        s_lo = jnp.where(mask_lo, score(q, below[h, 0]), NEG_BIG)
        s_hi = jnp.where(mask_hi, score(q, above[h, 0]), NEG_BIG)
        top = jnp.max(jnp.maximum(jnp.maximum(s_lo, s_hi), s_own), axis=1, keepdims=True)
        p_lo = jnp.exp(s_lo - top)
        p_own = jnp.exp(s_own - top)
        p_hi = jnp.exp(s_hi - top)
        total = jnp.sum(p_lo + p_own + p_hi, axis=1, keepdims=True)
        weighted = (
            jnp.dot(p_own.astype(jnp.bfloat16), kv_buf[1, :, cols], preferred_element_type=jnp.float32)
            + jnp.dot(p_lo.astype(jnp.bfloat16), below[h, 1], preferred_element_type=jnp.float32)
            + jnp.dot(p_hi.astype(jnp.bfloat16), above[h, 1], preferred_element_type=jnp.float32)
        )
        result = (weighted / total).astype(jnp.bfloat16).reshape(spans, mps, rows, HD)
        for xb in range(spans):
            for mb in range(mps):
                att[lax.rem(mb - m + mps, mps), lax.rem(xb - x + spans, spans), :, cols] = result[xb, mb]

    @pl.when((s > 0) & (s < last))
    def _():
        pl.semaphore_wait(relay, 1)
        pl.semaphore_signal(relay, 1, device_id={"section": succ})

    @pl.when(s == last)
    def _():
        pl.semaphore_wait(relay, 1)

    for load in loads[2:]:
        load.wait()
    level = level_ref[0]

    def to_mp(j, c):
        return pltpu.make_async_remote_copy(
            send_mp.at[j - 1, c], recv_mp.at[j - 1, c], mp_send.at[j - 1, c], mp_recv.at[j - 1, c],
            device_id={"mp": lax.rem(m + j, mps)},
        )

    def to_span(i, c):
        return pltpu.make_async_remote_copy(
            send_span.at[i - 1, c], recv_span.at[i - 1, c],
            span_send.at[i - 1, c], span_recv.at[i - 1, c],
            device_id={"span": lax.rem(x + i, spans)},
        )

    def to_next(c):
        return pltpu.make_async_remote_copy(
            send_next.at[c], out_hbm.at[0, :, chunk_cols(c)], next_send.at[c], next_recv.at[c],
            device_id={"section": succ},
        )

    def project(c):
        part = jnp.dot(
            att[...].reshape(tokens, width), w_buf[:, chunk_cols(c)],
            preferred_element_type=jnp.float32,
        ).reshape(mps, spans, rows, chunk)
        for j in range(1, mps):
            send_mp[j - 1, c] = part[j].astype(jnp.bfloat16)
            to_mp(j, c).start()
        keep[c] = part[0]

    def reduce_mp(c):
        total = keep[c]
        for j in range(1, mps):
            to_mp(j, c).wait_recv()
            total = total + recv_mp[j - 1, c].astype(jnp.float32)
        for i in range(1, spans):
            send_span[i - 1, c] = total[i].astype(jnp.bfloat16)
            to_span(i, c).start()
        keep[c, 0] = total[0]

    def finish(c):
        total = keep[c, 0]
        for i in range(1, spans):
            to_span(i, c).wait_recv()
            total = total + recv_span[i - 1, c].astype(jnp.float32)
        table = gate_buf[:, chunk_cols(c)]
        level_ids = lax.broadcasted_iota(jnp.int32, table.shape, 0)
        gate = jnp.sum(jnp.where(level_ids == level, table, 0.0), axis=0, keepdims=True)
        updated = lat_buf[:, chunk_cols(c)].astype(jnp.float32) + gate * total
        send_next[c] = updated.astype(jnp.bfloat16)
        to_next(c).start()

    @pl.loop(0, chunks + lag_span)
    def _(step):
        @pl.when(step < chunks)
        def _():
            project(step)

        @pl.when((step >= lag_mp) & (step < chunks + lag_mp))
        def _():
            reduce_mp(step - lag_mp)

        @pl.when(step >= lag_span)
        def _():
            finish(step - lag_span)

    @pl.loop(0, heads)
    def _(h):
        @pl.when(s < last)
        def _():
            up(h).wait_send()

        @pl.when(s > 0)
        def _():
            down(h).wait_send()

    @pl.loop(0, chunks)
    def _(c):
        for j in range(1, mps):
            to_mp(j, c).wait_send()
        for i in range(1, spans):
            to_span(i, c).wait_send()
        to_next(c).wait()


def shards(sizes, queries, keys_values, latents, out_weight, gate_table, level_index, pair_window):
    sections, spans, mps = sizes
    tokens, width = queries.shape[1:]
    rows, model = latents.shape[1:]
    heads = width // HD
    chunk = CHUNK if model % CHUNK == 0 else HD
    chunks = model // chunk
    bf16, f32 = jnp.bfloat16, jnp.float32
    dma = pltpu.SemaphoreType.DMA
    hbm = pl.BlockSpec(memory_space=pltpu.HBM)
    return pl.pallas_call(
        functools.partial(fused, sections, spans, mps, chunk, LAG_MP, LAG_SPAN),
        out_shape=jax.ShapeDtypeStruct(latents.shape, bf16),
        in_specs=[hbm, hbm, hbm, hbm, hbm, hbm, hbm],
        out_specs=hbm,
        scratch_shapes=[
            pltpu.VMEM((tokens, width), bf16),
            pltpu.VMEM((2, tokens, width), bf16),
            pltpu.VMEM((rows, model), bf16),
            pltpu.VMEM(out_weight.shape, bf16),
            pltpu.VMEM(gate_table.shape, f32),
            pltpu.VMEM((heads, 2, tokens, HD), bf16),
            pltpu.VMEM((heads, 2, tokens, HD), bf16),
            pltpu.VMEM((mps, spans, rows, width), bf16),
            pltpu.VMEM((chunks, spans, rows, chunk), f32),
            pltpu.VMEM((mps - 1, chunks, spans, rows, chunk), bf16),
            pltpu.VMEM((mps - 1, chunks, spans, rows, chunk), bf16),
            pltpu.VMEM((spans - 1, chunks, rows, chunk), bf16),
            pltpu.VMEM((spans - 1, chunks, rows, chunk), bf16),
            pltpu.VMEM((chunks, rows, chunk), bf16),
            pltpu.SMEM(level_index.shape, jnp.int32),
            pltpu.SMEM(pair_window.shape, jnp.int32),
            dma((7,)),
            dma((heads,)), dma((heads,)), dma((heads,)), dma((heads,)),
            dma((mps - 1, chunks)), dma((mps - 1, chunks)),
            dma((spans - 1, chunks)), dma((spans - 1, chunks)),
            dma((chunks,)), dma((chunks,)),
            pltpu.SemaphoreType.REGULAR,
        ],
        compiler_params=pltpu.CompilerParams(
            collective_id=0, has_side_effects=True, vmem_limit_bytes=60 * 1024 * 1024
        ),
    )(level_index, pair_window, queries, keys_values, latents, out_weight, gate_table)


def solution(mesh):
    sizes = (mesh.shape["section"], mesh.shape["span"], mesh.shape["mp"])
    in_specs = (
        P(("group", "section"), None, ("span", "mp")),
        P(None, ("group", "section"), None, ("span", "mp")),
        P(("group", "section"), ("span", "mp"), None),
        P(("span", "mp"), None),
        P(),
        P(("group", "section")),
        P("group"),
    )
    out_specs = P(("group", "section"), ("span", "mp"), None)
    return jax.shard_map(
        functools.partial(shards, sizes), mesh=mesh, in_specs=in_specs, out_specs=out_specs,
        check_vma=False,
    )
```

profile of v0, /device:TPU:0, one launch (start us, length us, event | category | flops | bytes accessed | tf_op | source)
XLA Modules:
  0.0 57.0 jit_solution(17587176295551845929)
XLA Ops:
  0.7 54.4 %shard_map.73 = bf16[1,64,5120]{2,1,0:T(8,128)(2,1)} custom-call(s32[1]{0:T(128)S(6)} %copy.9.level_hbm, s32[3]{0:T(128)} %window_hbm.1, bf16[1,256,1024]{2,1,0:T(8,128)(2,1)} %q_hbm.1, bf16[2,1,256,1024]{3,2,1,0:T(8,128)(2,1)} %kv_hbm.1, bf16[1,64,5120]{2,1,0:T(8,128)(2,1)} %lat_hbm.1, bf16[1024,5120]{1,0:T(8,128)(2,1)} %w_hbm.1, f32[8,5120]{1,0:T(8,128)} %gate_hbm.1), custom_call_target="tpu_custom_call" | custom-call | tf_op jit(solution)/shard_map/pallas_call | solution.py:269
  55.0 2.0 %copy.10 = bf16[1,64,5120]{2,1,0:T(8,128)(2,1)} copy(bf16[1,64,5120]{2,1,0:T(8,128)(2,1)} %shard_map.73) | data formatting | bytes 1310720
where the time goes:
time: 57.2 us; the launch traced here: 57 us
  Pallas kernels  54.4 us (95%)
  local copies, waits for them, and re-layouts  1.97 us (3%)
  between operations  0.66 us (1%)
    pallas_call x1, Pallas kernels, shards(): pl.pallas_call(functools.partial(fused, sections, spans, mps, chunk, LAG_...  54.4 us
    unnamed x1, local copies, waits for them, and re-layouts  1.97 us

commit v1 on v0

v1 whole, which is shorter than its diff:
```python
import functools
import math

import jax
import jax.numpy as jnp
from jax import lax
from jax.experimental import pallas as pl
from jax.experimental.pallas import tpu as pltpu
from jax.sharding import PartitionSpec as P

HD = 128
NEG_BIG = -1e30
BLOCKS = 2
CHUNK = 512
LAG_MP = 3
LAG_SPAN = 7
LANES = 128


def fused(
    sections, spans, mps, blocks, chunk, lag_mp, lag_span,
    level_hbm, window_hbm, q_hbm, kv_hbm, lat_hbm, w_hbm, gate_hbm, out_hbm,
    q_buf, kv_buf, lat_buf, w_buf, gate_buf, q_in, o_out, o_in, lse_out, lse_in, own, lse_own, att, keep,
    send_mp, recv_mp, send_span, recv_span, send_next,
    level_ref, window_ref, load_sems, q_send, q_recv, o_send, o_recv, lse_send, lse_recv,
    mp_send, mp_recv, span_send, span_recv, next_send, next_recv, relay,
):
    s = lax.axis_index("section")
    x = lax.axis_index("span")
    m = lax.axis_index("mp")
    last = sections - 1
    owners, rows, width = q_buf.shape
    tokens = kv_buf.shape[1]
    heads = width // HD
    piece = rows // blocks
    group = owners * piece
    stat_rows = lse_out.shape[2]
    chunks = w_buf.shape[1] // chunk
    steps = blocks * chunks
    succ = lax.rem(s + 1, sections)
    pred = lax.rem(s + sections - 1, sections)

    barrier = pltpu.get_barrier_semaphore()

    @pl.when(s < last)
    def _():
        pl.semaphore_signal(barrier, 1, device_id={"section": succ})

    @pl.when(s > 0)
    def _():
        pl.semaphore_signal(barrier, 1, device_id={"section": pred})

    for j in range(1, mps):
        pl.semaphore_signal(barrier, 1, device_id={"mp": lax.rem(m + j, mps)})
    for i in range(1, spans):
        pl.semaphore_signal(barrier, 1, device_id={"span": lax.rem(x + i, spans)})
    others = mps - 1 + spans - 1

    windows = pltpu.make_async_copy(window_hbm, window_ref, load_sems.at[6])
    loads = [
        pltpu.make_async_copy(q_hbm, q_buf, load_sems.at[0]),
        pltpu.make_async_copy(kv_hbm.at[:, 0], kv_buf, load_sems.at[1]),
        pltpu.make_async_copy(lat_hbm.at[0], lat_buf, load_sems.at[2]),
        pltpu.make_async_copy(gate_hbm, gate_buf, load_sems.at[3]),
        pltpu.make_async_copy(w_hbm, w_buf, load_sems.at[4]),
        pltpu.make_async_copy(level_hbm, level_ref, load_sems.at[5]),
    ]

    @pl.when((s > 0) & (s < last))
    def _():
        pl.semaphore_wait(barrier, others + 2)

    @pl.when((s == 0) | (s == last))
    def _():
        pl.semaphore_wait(barrier, others + 1)

    def head_cols(h):
        return pl.ds(pl.multiple_of(h * HD, HD), HD)

    def chunk_cols(c):
        return pl.ds(pl.multiple_of(c * chunk, chunk), chunk)

    def piece_rows(b):
        return pl.ds(pl.multiple_of(b * piece, piece), piece)

    def to_side(side, src, dst, send, recv):
        return pltpu.make_async_remote_copy(
            src, dst, send, recv, device_id={"section": succ if side == 0 else pred}
        )

    def ask(side, b, h):
        return to_side(
            side, q_hbm.at[:, piece_rows(b), head_cols(h)], q_in.at[side, b, :, :, head_cols(h)],
            q_send.at[side, b, h], q_recv.at[side, b, h],
        )

    def reply(side, b, h):
        return to_side(
            side, o_out.at[1 - side, b, h], o_in.at[side, b, h], o_send.at[side, b, h], o_recv.at[side, b, h]
        )

    def reply_lse(side, b):
        return to_side(
            side, lse_out.at[1 - side, b], lse_in.at[side, b, pl.ds(0, stat_rows)],
            lse_send.at[side, b], lse_recv.at[side, b],
        )

    sends_to = [s < last, s > 0]
    hears_from = [s > 0, s < last]

    for b in range(blocks):
        @pl.loop(0, heads)
        def _(h):
            for side in range(2):
                @pl.when(sends_to[side])
                def _():
                    ask(side, b, h).start()

    windows.start()
    for load in loads:
        load.start()

    @pl.when(s == 0)
    def _():
        pl.semaphore_signal(relay, 1, device_id={"section": succ})

    lse_own[...] = jnp.zeros_like(lse_own)
    for side in range(2):
        lse_in[side, :, stat_rows:] = jnp.full((blocks, LANES - stat_rows, group), NEG_BIG, jnp.float32)

        @pl.when(jnp.logical_not(hears_from[side]))
        def _():
            lse_in[side, :, :stat_rows] = jnp.full((blocks, stat_rows, group), NEG_BIG, jnp.float32)
            o_in[side] = jnp.zeros(o_in.shape[1:], o_in.dtype)

    windows.wait()
    pairs = window_ref.shape[0]
    w_lo = jnp.where(s > 0, window_ref[jnp.clip(s - 1, 0, pairs - 1)], 0)
    w_hi = jnp.where(s < last, window_ref[jnp.clip(s, 0, pairs - 1)], 0)
    scale = 1.0 / math.sqrt(HD)
    loads[0].wait()
    loads[1].wait()

    def attend(q, h, mask):
        cols = head_cols(h)
        scores = lax.dot_general(
            q, kv_buf[0, :, cols], (((1,), (1,)), ((), ())), preferred_element_type=jnp.float32
        ) * scale
        if mask is not None:
            scores = jnp.where(mask, scores, NEG_BIG)
        top = jnp.max(scores, axis=1, keepdims=True)
        probs = jnp.exp(scores - top)
        total = jnp.sum(probs, axis=1, keepdims=True)
        weighted = jnp.dot(probs.astype(jnp.bfloat16), kv_buf[1, :, cols], preferred_element_type=jnp.float32)
        return weighted * (1.0 / total), top + jnp.log(total)

    @pl.loop(0, heads)
    def _(h):
        cols = head_cols(h)
        lane = lax.broadcasted_iota(jnp.int32, (1, LANES), 1)
        for b in range(blocks):
            q = q_buf[:, piece_rows(b), cols].reshape(group, HD)
            value, lse = attend(q, h, None)
            own[b, :, cols] = value
            lse_own[b] = jnp.where(lane == h, lse, lse_own[b])

    lane = lax.broadcasted_iota(jnp.int32, (1, LANES), 1)
    key_ids = lax.broadcasted_iota(jnp.int32, (2 * group, tokens), 1)
    from_before = lax.broadcasted_iota(jnp.int32, (2 * group, tokens), 0) < group
    mask = jnp.where(from_before, key_ids, tokens - 1 - key_ids) < jnp.where(from_before, w_lo, w_hi)
    for b in range(blocks):
        def one_head(h, stats):
            for side in range(2):
                @pl.when(hears_from[side])
                def _():
                    ask(side, b, h).wait_recv()
            q = q_in[:, b, :, :, head_cols(h)].reshape(2 * group, HD)
            value, lse = attend(q, h, mask)
            value = value.astype(jnp.bfloat16).reshape(2, group, HD)
            for side in range(2):
                o_out[side, b, h] = value[side]
            for side in range(2):
                @pl.when(sends_to[side])
                def _():
                    reply(side, b, h).start()
            return jnp.where(lane == h, lse, stats)

        stats = lax.fori_loop(0, heads, one_head, jnp.zeros((2 * group, LANES), jnp.float32))
        for side in range(2):
            lse_out[side, b] = stats[side * group:(side + 1) * group].T[:stat_rows]
        for side in range(2):
            @pl.when(sends_to[side])
            def _():
                reply_lse(side, b).start()

    @pl.when((s > 0) & (s < last))
    def _():
        pl.semaphore_wait(relay, 1)
        pl.semaphore_signal(relay, 1, device_id={"section": succ})

    @pl.when(s == last)
    def _():
        pl.semaphore_wait(relay, 1)

    for load in loads[2:]:
        load.wait()
    level = level_ref[0]

    def to_mp(j, t):
        return pltpu.make_async_remote_copy(
            send_mp.at[j - 1, t], recv_mp.at[j - 1, t], mp_send.at[j - 1, t], mp_recv.at[j - 1, t],
            device_id={"mp": lax.rem(m + j, mps)},
        )

    def to_span(i, t):
        return pltpu.make_async_remote_copy(
            send_span.at[i - 1, t], recv_span.at[i - 1, t],
            span_send.at[i - 1, t], span_recv.at[i - 1, t],
            device_id={"span": lax.rem(x + i, spans)},
        )

    def to_next(t):
        return pltpu.make_async_remote_copy(
            send_next.at[t], out_hbm.at[0, piece_rows(t // chunks), chunk_cols(t % chunks)],
            next_send.at[t], next_recv.at[t], device_id={"section": succ},
        )

    def combine(b):
        @pl.loop(0, heads)
        def _(h):
            for side in range(2):
                @pl.when(hears_from[side])
                def _():
                    reply(side, b, h).wait_recv()

        for side in range(2):
            @pl.when(hears_from[side])
            def _():
                reply_lse(side, b).wait_recv()

        parts = [lse_own[b], lse_in[0, b].T, lse_in[1, b].T]
        top = jnp.maximum(jnp.maximum(parts[0], parts[1]), parts[2])
        parts = [jnp.exp(part - top) for part in parts]
        total = 1.0 / (parts[0] + parts[1] + parts[2])
        parts = [part * total for part in parts]
        for h in range(heads):
            cols = slice(h * HD, (h + 1) * HD)
            shares = [part[:, h:h + 1] for part in parts]
            result = own[b, :, cols] * shares[0]
            for side in range(2):
                result = result + o_in[side, b, h].astype(jnp.float32) * shares[side + 1]
            result = result.astype(jnp.bfloat16).reshape(spans, mps, piece, HD)
            for xb in range(spans):
                for mb in range(mps):
                    att[b, lax.rem(mb - m + mps, mps), lax.rem(xb - x + spans, spans), :, cols] = result[xb, mb]

    def project(t):
        part = jnp.dot(
            att[t // chunks].reshape(group, width), w_buf[:, chunk_cols(t % chunks)],
            preferred_element_type=jnp.float32,
        ).reshape(mps, spans, piece, chunk)
        for j in range(1, mps):
            send_mp[j - 1, t] = part[j].astype(jnp.bfloat16)
            to_mp(j, t).start()
        keep[t] = part[0]

    def reduce_mp(t):
        total = keep[t]
        for j in range(1, mps):
            to_mp(j, t).wait_recv()
            total = total + recv_mp[j - 1, t].astype(jnp.float32)
        for i in range(1, spans):
            send_span[i - 1, t] = total[i].astype(jnp.bfloat16)
            to_span(i, t).start()
        keep[t, 0] = total[0]

    def finish(t):
        total = keep[t, 0]
        for i in range(1, spans):
            to_span(i, t).wait_recv()
            total = total + recv_span[i - 1, t].astype(jnp.float32)
        table = gate_buf[:, chunk_cols(t % chunks)]
        level_ids = lax.broadcasted_iota(jnp.int32, table.shape, 0)
        gate = jnp.sum(jnp.where(level_ids == level, table, 0.0), axis=0, keepdims=True)
        updated = lat_buf[piece_rows(t // chunks), chunk_cols(t % chunks)].astype(jnp.float32) + gate * total
        send_next[t] = updated.astype(jnp.bfloat16)
        to_next(t).start()

    @pl.loop(0, steps + lag_span)
    def _(step):
        for b in range(blocks):
            @pl.when(step == b * chunks)
            def _():
                combine(b)

        @pl.when(step < steps)
        def _():
            project(step)

        @pl.when((step >= lag_mp) & (step < steps + lag_mp))
        def _():
            reduce_mp(step - lag_mp)

        @pl.when(step >= lag_span)
        def _():
            finish(step - lag_span)

    for b in range(blocks):
        @pl.loop(0, heads)
        def _(h):
            for side in range(2):
                @pl.when(sends_to[side])
                def _():
                    ask(side, b, h).wait_send()
                    reply(side, b, h).wait_send()

        for side in range(2):
            @pl.when(sends_to[side])
            def _():
                reply_lse(side, b).wait_send()

    @pl.loop(0, steps)
    def _(t):
        for j in range(1, mps):
            to_mp(j, t).wait_send()
        for i in range(1, spans):
            to_span(i, t).wait_send()
        to_next(t).wait()


def shards(sizes, queries, keys_values, latents, out_weight, gate_table, level_index, pair_window):
    sections, spans, mps = sizes
    tokens, width = queries.shape[1:]
    rows, model = latents.shape[1:]
    heads = width // HD
    owners = spans * mps
    blocks = BLOCKS
    piece = rows // blocks
    group = owners * piece
    stat_rows = -(-heads // 8) * 8
    chunk = CHUNK if model % CHUNK == 0 else HD
    steps = blocks * (model // chunk)
    bf16, f32 = jnp.bfloat16, jnp.float32
    dma = pltpu.SemaphoreType.DMA
    hbm = pl.BlockSpec(memory_space=pltpu.HBM)
    return pl.pallas_call(
        functools.partial(fused, sections, spans, mps, blocks, chunk, LAG_MP, LAG_SPAN),
        out_shape=jax.ShapeDtypeStruct(latents.shape, bf16),
        in_specs=[hbm, hbm, hbm, hbm, hbm, hbm, hbm],
        out_specs=hbm,
        scratch_shapes=[
            pltpu.VMEM((owners, rows, width), bf16),
            pltpu.VMEM((2, tokens, width), bf16),
            pltpu.VMEM((rows, model), bf16),
            pltpu.VMEM(out_weight.shape, bf16),
            pltpu.VMEM(gate_table.shape, f32),
            pltpu.VMEM((2, blocks, owners, piece, width), bf16),
            pltpu.VMEM((2, blocks, heads, group, HD), bf16),
            pltpu.VMEM((2, blocks, heads, group, HD), bf16),
            pltpu.VMEM((2, blocks, stat_rows, group), f32),
            pltpu.VMEM((2, blocks, LANES, group), f32),
            pltpu.VMEM((blocks, group, width), f32),
            pltpu.VMEM((blocks, group, LANES), f32),
            pltpu.VMEM((blocks, mps, spans, piece, width), bf16),
            pltpu.VMEM((steps, spans, piece, chunk), f32),
            pltpu.VMEM((mps - 1, steps, spans, piece, chunk), bf16),
            pltpu.VMEM((mps - 1, steps, spans, piece, chunk), bf16),
            pltpu.VMEM((spans - 1, steps, piece, chunk), bf16),
            pltpu.VMEM((spans - 1, steps, piece, chunk), bf16),
            pltpu.VMEM((steps, piece, chunk), bf16),
            pltpu.SMEM(level_index.shape, jnp.int32),
            pltpu.SMEM(pair_window.shape, jnp.int32),
            dma((7,)),
            dma((2, blocks, heads)), dma((2, blocks, heads)),
            dma((2, blocks, heads)), dma((2, blocks, heads)),
            dma((2, blocks)), dma((2, blocks)),
            dma((mps - 1, steps)), dma((mps - 1, steps)),
            dma((spans - 1, steps)), dma((spans - 1, steps)),
            dma((steps,)), dma((steps,)),
            pltpu.SemaphoreType.REGULAR,
        ],
        compiler_params=pltpu.CompilerParams(
            collective_id=0, has_side_effects=True, vmem_limit_bytes=60 * 1024 * 1024
        ),
    )(level_index, pair_window, queries.reshape(owners, rows, width), keys_values, latents, out_weight, gate_table)


def solution(mesh):
    sizes = (mesh.shape["section"], mesh.shape["span"], mesh.shape["mp"])
    in_specs = (
        P(("group", "section"), None, ("span", "mp")),
        P(None, ("group", "section"), None, ("span", "mp")),
        P(("group", "section"), ("span", "mp"), None),
        P(("span", "mp"), None),
        P(),
        P(("group", "section")),
        P("group"),
    )
    out_specs = P(("group", "section"), ("span", "mp"), None)
    return jax.shard_map(
        functools.partial(shards, sizes), mesh=mesh, in_specs=in_specs, out_specs=out_specs,
        check_vma=False,
    )
```

time: 57.2 us -> 51.9 us (0.907)
  Pallas kernels: 54.4 us -> 49.1 us
    pallas_call x1, Pallas kernels: 54.4 us -> 49.1 us  [shards(): pl.pallas_call(functools.partial(fused, sections, spans, mps, blocks, chu...]
where the time goes in v1:
time: 51.9 us; the launch traced here: 51.8 us
  Pallas kernels  49.1 us (95%)
  local copies, waits for them, and re-layouts  1.97 us (4%)
  between operations  0.66 us (1%)
    pallas_call x1, Pallas kernels, shards(): pl.pallas_call(functools.partial(fused, sections, spans, mps, blocks, chu...  49.1 us
    unnamed x1, local copies, waits for them, and re-layouts  1.97 us

profile of v1, /device:TPU:0, one launch (start us, length us, event | category | flops | bytes accessed | tf_op | source)
XLA Modules:
  0.0 51.8 jit_solution(7077809783919638587)
XLA Ops:
  0.7 49.1 %shard_map.73 = bf16[1,64,5120]{2,1,0:T(8,128)(2,1)} custom-call(s32[1]{0:T(128)S(6)} %copy.9.level_hbm, s32[3]{0:T(128)} %window_hbm.1, bf16[4,64,1024]{2,1,0:T(8,128)(2,1)} %bitcast.1, bf16[2,1,256,1024]{3,2,1,0:T(8,128)(2,1)} %kv_hbm.1, bf16[1,64,5120]{2,1,0:T(8,128)(2,1)} %lat_hbm.1, bf16[1024,5120]{1,0:T(8,128)(2,1)} %w_hbm.1, f32[8,5120]{1,0:T(8,128)} %gate_hbm.1), custom_call_target="tpu_custom_call" | custom-call | tf_op jit(solution)/shard_map/pallas_call | solution.py:346
  49.8 2.0 %copy.10 = bf16[1,64,5120]{2,1,0:T(8,128)(2,1)} copy(bf16[1,64,5120]{2,1,0:T(8,128)(2,1)} %shard_map.73) | data formatting | bytes 1310720

commit v2 on v1

--- a/solution.py
+++ b/solution.py
@@ -12,15 +12,16 @@
 NEG_BIG = -1e30
 BLOCKS = 2
 CHUNK = 512
-LAG_MP = 3
-LAG_SPAN = 7
+LAG_MP = 2
+LAG_SPAN = 6
+LATE_STEP = 2
 LANES = 128
 
 
 def fused(
-    sections, spans, mps, blocks, chunk, lag_mp, lag_span,
+    sections, spans, mps, blocks, chunk, lag_mp, lag_span, late_step,
     level_hbm, window_hbm, q_hbm, kv_hbm, lat_hbm, w_hbm, gate_hbm, out_hbm,
-    q_buf, kv_buf, lat_buf, w_buf, gate_buf, q_in, o_out, o_in, lse_out, lse_in, own, lse_own, att, keep,
+    q_buf, kv_buf, lat_buf, w_buf, gate_buf, q_in, o_out, o_in, lse_out, lse_in, own, lse_own, stats, att, keep,
     send_mp, recv_mp, send_span, recv_span, send_next,
     level_ref, window_ref, load_sems, q_send, q_recv, o_send, o_recv, lse_send, lse_recv,
     mp_send, mp_recv, span_send, span_recv, next_send, next_recv, relay,
@@ -66,6 +67,10 @@
         pltpu.make_async_copy(level_hbm, level_ref, load_sems.at[5]),
     ]
 
+    windows.start()
+    for load in loads:
+        load.start()
+
     @pl.when((s > 0) & (s < last))
     def _():
         pl.semaphore_wait(barrier, others + 2)
@@ -108,23 +113,25 @@
     sends_to = [s < last, s > 0]
     hears_from = [s > 0, s < last]
 
-    for b in range(blocks):
-        @pl.loop(0, heads)
+    def ask_all(b, first, end):
+        @pl.loop(first, end)
         def _(h):
             for side in range(2):
                 @pl.when(sends_to[side])
                 def _():
                     ask(side, b, h).start()
 
-    windows.start()
-    for load in loads:
-        load.start()
+    early = heads // 2
+    late = heads - early
+    ask_all(0, 0, heads)
+    ask_all(1, 0, early)
 
     @pl.when(s == 0)
     def _():
         pl.semaphore_signal(relay, 1, device_id={"section": succ})
 
     lse_own[...] = jnp.zeros_like(lse_own)
+    stats[...] = jnp.zeros_like(stats)
     for side in range(2):
         lse_in[side, :, stat_rows:] = jnp.full((blocks, LANES - stat_rows, group), NEG_BIG, jnp.float32)
 
@@ -164,34 +171,45 @@
             own[b, :, cols] = value
             lse_own[b] = jnp.where(lane == h, lse, lse_own[b])
 
-    lane = lax.broadcasted_iota(jnp.int32, (1, LANES), 1)
-    key_ids = lax.broadcasted_iota(jnp.int32, (2 * group, tokens), 1)
-    from_before = lax.broadcasted_iota(jnp.int32, (2 * group, tokens), 0) < group
-    mask = jnp.where(from_before, key_ids, tokens - 1 - key_ids) < jnp.where(from_before, w_lo, w_hi)
-    for b in range(blocks):
-        def one_head(h, stats):
-            for side in range(2):
-                @pl.when(hears_from[side])
-                def _():
-                    ask(side, b, h).wait_recv()
-            q = q_in[:, b, :, :, head_cols(h)].reshape(2 * group, HD)
-            value, lse = attend(q, h, mask)
-            value = value.astype(jnp.bfloat16).reshape(2, group, HD)
-            for side in range(2):
-                o_out[side, b, h] = value[side]
-            for side in range(2):
-                @pl.when(sends_to[side])
-                def _():
-                    reply(side, b, h).start()
-            return jnp.where(lane == h, lse, stats)
-
-        stats = lax.fori_loop(0, heads, one_head, jnp.zeros((2 * group, LANES), jnp.float32))
-        for side in range(2):
-            lse_out[side, b] = stats[side * group:(side + 1) * group].T[:stat_rows]
+    def mask():
+        key_ids = lax.broadcasted_iota(jnp.int32, (2 * group, tokens), 1)
+        from_before = lax.broadcasted_iota(jnp.int32, (2 * group, tokens), 0) < group
+        return jnp.where(from_before, key_ids, tokens - 1 - key_ids) < jnp.where(from_before, w_lo, w_hi)
+
+    def answer(b, h):
+        for side in range(2):
+            @pl.when(hears_from[side])
+            def _():
+                ask(side, b, h).wait_recv()
+        q = q_in[:, b, :, :, head_cols(h)].reshape(2 * group, HD)
+        value, lse = attend(q, h, mask())
+        value = value.astype(jnp.bfloat16).reshape(2, group, HD)
+        for side in range(2):
+            o_out[side, b, h] = value[side]
         for side in range(2):
             @pl.when(sends_to[side])
             def _():
+                reply(side, b, h).start()
+        stats[b] = jnp.where(lax.broadcasted_iota(jnp.int32, (1, LANES), 1) == h, lse, stats[b])
+
+    def answer_lse(b):
+        for side in range(2):
+            lse_out[side, b] = stats[b, side * group:(side + 1) * group].T[:stat_rows]
+        for side in range(2):
+            @pl.when(sends_to[side])
+            def _():
                 reply_lse(side, b).start()
+
+    @pl.loop(0, heads)
+    def _(h):
+        answer(0, h)
+
+    answer_lse(0)
+    ask_all(1, early, heads)
+
+    @pl.loop(0, early)
+    def _(h):
+        answer(1, h)
 
     @pl.when((s > 0) & (s < last))
     def _():
@@ -304,6 +322,14 @@
         @pl.when(step >= lag_span)
         def _():
             finish(step - lag_span)
+
+        @pl.when((step >= late_step) & (step < late_step + late))
+        def _():
+            answer(1, early + step - late_step)
+
+        @pl.when(step == late_step + late - 1)
+        def _():
+            answer_lse(1)
 
     for b in range(blocks):
         @pl.loop(0, heads)
@@ -344,7 +370,7 @@
     dma = pltpu.SemaphoreType.DMA
     hbm = pl.BlockSpec(memory_space=pltpu.HBM)
     return pl.pallas_call(
-        functools.partial(fused, sections, spans, mps, blocks, chunk, LAG_MP, LAG_SPAN),
+        functools.partial(fused, sections, spans, mps, blocks, chunk, LAG_MP, LAG_SPAN, LATE_STEP),
         out_shape=jax.ShapeDtypeStruct(latents.shape, bf16),
         in_specs=[hbm, hbm, hbm, hbm, hbm, hbm, hbm],
         out_specs=hbm,
@@ -361,6 +387,7 @@
             pltpu.VMEM((2, blocks, LANES, group), f32),
             pltpu.VMEM((blocks, group, width), f32),
             pltpu.VMEM((blocks, group, LANES), f32),
+            pltpu.VMEM((blocks, 2 * group, LANES), f32),
             pltpu.VMEM((blocks, mps, spans, piece, width), bf16),
             pltpu.VMEM((steps, spans, piece, chunk), f32),
             pltpu.VMEM((mps - 1, steps, spans, piece, chunk), bf16),

time: 51.9 us -> 49.9 us (0.961)
  Pallas kernels: 49.1 us -> 47.1 us
    pallas_call x1, Pallas kernels: 49.1 us -> 47.1 us  [shards(): pl.pallas_call(functools.partial(fused, sections, spans, mps, blocks, chu...]
where the time goes in v2:
time: 49.9 us; the launch traced here: 49.7 us
  Pallas kernels  47.1 us (94%)
  local copies, waits for them, and re-layouts  1.97 us (4%)
  between operations  0.66 us (1%)
    pallas_call x1, Pallas kernels, shards(): pl.pallas_call(functools.partial(fused, sections, spans, mps, blocks, chu...  47.1 us
    unnamed x1, local copies, waits for them, and re-layouts  1.97 us

profile of v2, /device:TPU:0, one launch (start us, length us, event | category | flops | bytes accessed | tf_op | source)
XLA Modules:
  0.0 49.7 jit_solution(6037144296493634102)
XLA Ops:
  0.7 47.1 %shard_map.73 = bf16[1,64,5120]{2,1,0:T(8,128)(2,1)} custom-call(s32[1]{0:T(128)S(6)} %copy.9.level_hbm, s32[3]{0:T(128)} %window_hbm.1, bf16[4,64,1024]{2,1,0:T(8,128)(2,1)} %bitcast.1, bf16[2,1,256,1024]{3,2,1,0:T(8,128)(2,1)} %kv_hbm.1, bf16[1,64,5120]{2,1,0:T(8,128)(2,1)} %lat_hbm.1, bf16[1024,5120]{1,0:T(8,128)(2,1)} %w_hbm.1, f32[8,5120]{1,0:T(8,128)} %gate_hbm.1), custom_call_target="tpu_custom_call" | custom-call | tf_op jit(solution)/shard_map/pallas_call | solution.py:372
  47.8 2.0 %copy.10 = bf16[1,64,5120]{2,1,0:T(8,128)(2,1)} copy(bf16[1,64,5120]{2,1,0:T(8,128)(2,1)} %shard_map.73) | data formatting | bytes 1310720
